TPU v7x, 32 devices: a whole 2x2x4 slice. The times are simulated.
32 devices in a mesh: dp: 16 (over z, y, core), tensor: 2 (over x).
Axes of the slice: x: 2, y: 2, z: 4, core: 2. Of those that a mesh axis runs over, the one named last changes fastest.
Arguments:
- block_input: bfloat16 [16384, 1536], P('dp'), may hold values from -50 to 50
- cotangent: bfloat16 [16384, 1536], P('dp'), may hold values from -6 to 6
- pre_gain: float32 [1536], replicated, may hold values from 0.5 to 1.5
- gate_proj: bfloat16 [1536, 3072], P(None, 'tensor'), may hold values from -0.15625 to 0.15625
- value_proj: bfloat16 [1536, 3072], P(None, 'tensor'), may hold values from -0.15625 to 0.15625
- step_proj: bfloat16 [1536, 48], P(None, 'tensor'), may hold values from -0.15625 to 0.15625
- state_proj: bfloat16 [1536, 256], replicated, may hold values from -0.15625 to 0.15625
- conv_value: float32 [4, 3072], P(None, 'tensor'), may hold values from -3 to 3
- conv_value_bias: float32 [3072], P('tensor'), may hold values from -3 to 3
- conv_state: float32 [4, 256], replicated, may hold values from -3 to 3
- conv_state_bias: float32 [256], replicated, may hold values from -3 to 3
- step_bias: float32 [48], P('tensor'), may hold values from -6.9 to -2.3
- decay_log: float32 [48], P('tensor'), may hold values from 0 to 2.77
- skip_gain: float32 [48], P('tensor'), may hold values from 0.5 to 1.5
- norm_gain: float32 [3072], P('tensor'), may hold values from 0.5 to 1.5
- out_proj: bfloat16 [3072, 1536], P('tensor'), may hold values from -0.109375 to 0.109375
Outputs:
- block_out: bfloat16 [16384, 1536], P('dp')
- grad_input: float32 [16384, 1536], P('dp')
- grad_pre_gain: float32 [1536], replicated
- grad_gate_proj: float32 [1536, 3072], P(None, 'tensor')
- grad_value_proj: float32 [1536, 3072], P(None, 'tensor')
- grad_step_proj: float32 [1536, 48], P(None, 'tensor')
- grad_state_proj: float32 [1536, 256], replicated
- grad_conv_value: float32 [4, 3072], P(None, 'tensor')
- grad_conv_value_bias: float32 [3072], P('tensor')
- grad_conv_state: float32 [4, 256], replicated
- grad_conv_state_bias: float32 [256], replicated
- grad_step_bias: float32 [48], P('tensor')
- grad_decay_log: float32 [48], P('tensor')
- grad_skip_gain: float32 [48], P('tensor')
- grad_norm_gain: float32 [3072], P('tensor')
- grad_out_proj: float32 [3072, 1536], P('tensor')
All inputs are finite; a program needn't handle non-finite values.
Results may differ from a plain program's by a relative error of at most 0.008.
Values may be sent and summed in bfloat16 or wider, within the bound.
No kernel may reach another device: no remote copies, remote signals or barrier semaphores. Data moves between devices by JAX's collectives and lax.ppermute only.
A program may use at most 256 MiB of HBM per device.

v0:
```python
import jax
import jax.numpy as jnp
from jax import lax
from jax.sharding import PartitionSpec as P

D = 1536
BLOCK = 256
SEQ_LEN = 1024
INNER = 3072
epsilon = 1e-05
highest = lax.Precision.HIGHEST


def causal_conv(values, kernel, offset):
    kernel_width = kernel.shape[0]
    length = values.shape[0]
    padded = jnp.concatenate(
        [jnp.zeros((kernel_width - 1, values.shape[1]), jnp.float32), values], axis=0
    )
    running_sum = jnp.zeros_like(values) + offset[None, :]
    for tap_index in range(kernel_width):
        running_sum = (
            running_sum + kernel[tap_index][None, :] * padded[tap_index : tap_index + length]
        )
    return running_sum


def make_states(bc_raw, conv_state, conv_state_bias):
    return jax.nn.silu(causal_conv(bc_raw, conv_state, conv_state_bias))


def mixer(
    conv_in,
    states,
    step_raw,
    gate_raw,
    conv_value,
    conv_value_bias,
    step_bias,
    decay_log,
    skip_gain,
):
    length = conv_in.shape[0]
    head_count = skip_gain.shape[0]
    head_width = conv_in.shape[1] // head_count
    state_width = states.shape[1] // 2
    block_count = length // BLOCK
    conv_out = jax.nn.silu(causal_conv(conv_in, conv_value, conv_value_bias))
    step_size = jax.nn.softplus(step_raw + step_bias[None, :])
    decay_rate = -jnp.exp(decay_log)
    log_decay = step_size * decay_rate[None, :]
    writer = states[:, :state_width].reshape(block_count, BLOCK, state_width)
    reader = states[:, state_width:].reshape(block_count, BLOCK, state_width)
    head_values = conv_out.reshape(block_count, BLOCK, head_count, head_width)
    cumulative = jnp.cumsum(log_decay.reshape(block_count, BLOCK, head_count), axis=1)
    cum_heads = jnp.transpose(cumulative, (0, 2, 1))
    step_heads = jnp.transpose(step_size.reshape(block_count, BLOCK, head_count), (0, 2, 1))
    scores = jnp.einsum("ktn,ksn->kts", reader, writer, precision=highest)
    causal_mask = jnp.tril(jnp.ones((BLOCK, BLOCK), jnp.float32))
    log_gap = cum_heads[:, :, :, None] - cum_heads[:, :, None, :]
    decay = jnp.exp(jnp.where(causal_mask > 0, log_gap, 0.0)) * causal_mask
    weights = scores[:, None, :, :] * decay * step_heads[:, :, None, :]
    intra_part = jnp.einsum("khts,kshp->kthp", weights, head_values, precision=highest)
    tail_weight = jnp.exp(cum_heads[:, :, -1:] - cum_heads) * step_heads
    block_state = jnp.einsum(
        "ksn,khs,kshp->khnp", writer, tail_weight, head_values, precision=highest
    )
    block_fade = jnp.exp(cum_heads[:, :, -1])

    def advance(carried, item):
        new_part, keep_factor = item
        return (carried * keep_factor[:, None, None] + new_part, carried)

    initial = jnp.zeros((head_count, state_width, head_width), jnp.float32)
    _, entering = lax.scan(advance, initial, (block_state, block_fade))
    inter_part = (
        jnp.einsum("ktn,khnp->kthp", reader, entering, precision=highest)
        * jnp.exp(cumulative)[:, :, :, None]
    )
    mixed_out = intra_part + inter_part + skip_gain[None, None, :, None] * head_values
    mixed_out = mixed_out.reshape(length, head_count * head_width)
    return mixed_out * jax.nn.silu(gate_raw)


def dot_plain(left, right):
    return jnp.dot(left, right, preferred_element_type=jnp.float32)


def dot_inner(left, right):
    return lax.dot_general(
        left, right, (((0,), (0,)), ((), ())), preferred_element_type=jnp.float32
    )


def dot_outer(left, right):
    return lax.dot_general(
        left, right, (((1,), (1,)), ((), ())), preferred_element_type=jnp.float32
    )


def local(
    block_input,
    cotangent,
    pre_gain,
    gate_proj,
    value_proj,
    step_proj,
    state_proj,
    conv_value,
    conv_value_bias,
    conv_state,
    conv_state_bias,
    step_bias,
    decay_log,
    skip_gain,
    norm_gain,
    out_proj,
):
    row_count = block_input.shape[0]
    seq_count = row_count // SEQ_LEN

    def by_sequence(array):
        return array.reshape(seq_count, SEQ_LEN, array.shape[1])

    def by_row(array):
        return array.reshape(row_count, array.shape[2])

    input_f32 = block_input.astype(jnp.float32)
    pre_scale = lax.rsqrt(jnp.mean(input_f32 * input_f32, axis=1, keepdims=True) + epsilon)
    normed = (input_f32 * pre_scale * pre_gain[None, :]).astype(jnp.bfloat16)
    gate_raw = dot_plain(normed, gate_proj)
    conv_in = dot_plain(normed, value_proj)
    step_raw = dot_plain(normed, step_proj)
    bc_raw = dot_plain(normed, state_proj)
    states, state_back = jax.vjp(
        jax.vmap(make_states, in_axes=(0, None, None)),
        by_sequence(bc_raw),
        conv_state,
        conv_state_bias,
    )
    gated_seq, mixer_back = jax.vjp(
        jax.vmap(mixer, in_axes=(0, 0, 0, 0, None, None, None, None, None)),
        by_sequence(conv_in),
        states,
        by_sequence(step_raw),
        by_sequence(gate_raw),
        conv_value,
        conv_value_bias,
        step_bias,
        decay_log,
        skip_gain,
    )
    gated = by_row(gated_seq)
    square_sum = lax.psum(jnp.sum(gated * gated, axis=1), "tensor")
    gate_scale = lax.rsqrt(square_sum[:, None] / INNER + epsilon)
    gated_normed = (gated * gate_scale * norm_gain[None, :]).astype(jnp.bfloat16)
    branch = lax.psum(dot_plain(gated_normed, out_proj).astype(jnp.bfloat16), "tensor").astype(
        jnp.float32
    )
    block_out = (input_f32 + branch).astype(jnp.bfloat16)
    d_gn = dot_outer(cotangent, out_proj)
    grad_out_proj = dot_inner(gated_normed, cotangent)
    grad_norm_gain = jnp.sum(d_gn * gated * gate_scale, axis=0)
    gate_dot = lax.psum(jnp.sum(d_gn * norm_gain[None, :] * gated, axis=1), "tensor")
    d_gated = (
        gate_scale * norm_gain[None, :] * d_gn - gated * gate_scale**3 * gate_dot[:, None] / INNER
    )
    (
        d_conv_in,
        d_states,
        d_step_raw,
        d_gate_raw,
        grad_conv_value,
        grad_conv_value_bias,
        grad_step_bias,
        grad_decay_log,
        grad_skip_gain,
    ) = mixer_back(by_sequence(d_gated))
    state_total = lax.psum(by_row(d_states), "tensor")
    d_bc_raw, grad_conv_state, grad_conv_state_bias = state_back(by_sequence(state_total))
    gate_bf = by_row(d_gate_raw).astype(jnp.bfloat16)
    value_bf = by_row(d_conv_in).astype(jnp.bfloat16)
    step_bf = by_row(d_step_raw).astype(jnp.bfloat16)
    state_bf = by_row(d_bc_raw).astype(jnp.bfloat16)
    head_terms = (
        dot_outer(gate_bf, gate_proj)
        + dot_outer(value_bf, value_proj)
        + dot_outer(step_bf, step_proj)
    )
    d_normed = lax.psum(head_terms, "tensor") + dot_outer(state_bf, state_proj)
    grad_pre_gain = jnp.sum(d_normed * input_f32 * pre_scale, axis=0)
    pre_dot = jnp.sum(d_normed * pre_gain[None, :] * input_f32, axis=1, keepdims=True)
    grad_input = (
        cotangent.astype(jnp.float32)
        + pre_scale * pre_gain[None, :] * d_normed
        - input_f32 * pre_scale**3 * pre_dot / D
    )
    grad_gate_proj = dot_inner(normed, gate_bf)
    grad_value_proj = dot_inner(normed, value_bf)
    grad_step_proj = dot_inner(normed, step_bf)
    grad_state_proj = dot_inner(normed, state_bf)
    (
        grad_pre_gain,
        grad_gate_proj,
        grad_value_proj,
        grad_step_proj,
        grad_state_proj,
        grad_conv_value,
        grad_conv_value_bias,
        grad_conv_state,
        grad_conv_state_bias,
        grad_step_bias,
        grad_decay_log,
        grad_skip_gain,
        grad_norm_gain,
        grad_out_proj,
    ) = lax.psum(
        (
            grad_pre_gain,
            grad_gate_proj,
            grad_value_proj,
            grad_step_proj,
            grad_state_proj,
            grad_conv_value,
            grad_conv_value_bias,
            grad_conv_state,
            grad_conv_state_bias,
            grad_step_bias,
            grad_decay_log,
            grad_skip_gain,
            grad_norm_gain,
            grad_out_proj,
        ),
        "dp",
    )
    return (
        block_out,
        grad_input,
        grad_pre_gain,
        grad_gate_proj,
        grad_value_proj,
        grad_step_proj,
        grad_state_proj,
        grad_conv_value,
        grad_conv_value_bias,
        grad_conv_state,
        grad_conv_state_bias,
        grad_step_bias,
        grad_decay_log,
        grad_skip_gain,
        grad_norm_gain,
        grad_out_proj,
    )


def solution(mesh):
    placed = (
        P("dp", None),
        P("dp", None),
        P(),
        P(None, "tensor"),
        P(None, "tensor"),
        P(None, "tensor"),
        P(),
        P(None, "tensor"),
        P("tensor"),
        P(),
        P(),
        P("tensor"),
        P("tensor"),
        P("tensor"),
        P("tensor"),
        P("tensor", None),
    )
    return jax.shard_map(
        local,
        mesh=mesh,
        in_specs=placed,
        out_specs=(
            P("dp", None),
            P("dp", None),
            P(),
            P(None, "tensor"),
            P(None, "tensor"),
            P(None, "tensor"),
            P(),
            P(None, "tensor"),
            P("tensor"),
            P(),
            P(),
            P("tensor"),
            P("tensor"),
            P("tensor"),
            P("tensor"),
            P("tensor", None),
        ),
        check_vma=False,
    )
```

profile of v0, /device:TPU:0, one launch (start us, length us, event | category | flops | bytes accessed | tf_op | source)
XLA Modules:
  0.0 1340.4 jit_solution(6802195912920558726)
XLA Ops:
  42.9 10.0 reshape.687
  71.3 10.3 fusion.83
  85.1 23.3 %while.34 = (s32[]{:T(128)}, f32[1,24,128,64]{3,2,1,0:T(8,128)S(1)}, f32[4,1,24,128,64]{4,3,2,1,0:T(8,128)}, f32[4,1,24,1,1]{2,4,3,1,0:T(1,128)S(1)}, f32[4,1,24...) while((s32[]{:T(128)}, f32[1,24,128,64]{3,2,1,0:T(8,128)S(1)}, ...), condition=%wide.region_4.5_spmd.clone, body=%wide.region_3.4_spmd.clone.sunk | while | flops 786435 | bytes 7865752 | solution.py:75
  124.4 9.8 copy.207
  134.3 33.3 %fusion.42 = f32[1,4,256,24,64]{2,4,3,1,0:T(8,128)} fusion(f32[1,4,256,24,64]{2,4,3,1,0:T(8,128)} %copy.207, f32[4,256,24,64]{1,3,2,0:T(8,128)} %bitcast.279, f32[24]{0:T(128)S(1)} %copy-done.93, f32[4,256,24]{1,2,0:T(8,128)S(1)} %bitcast.300, f32[4,24,256]{2,1,0:T(8,128)S(1)} %copy-done.48, f32[256,256]{1,0:T(8,128)S(1)} %copy-done.42, ...), kind=kOutput, calls=%fused_computation.68 | convolution fusion | flops 4869586944 | bytes 26837088 | tf_op jit(solution)/shard_map/jvp(vmap(khts,kshp->kthp))/dot_general | solution.py:63
  177.3 11.1 reshape.688
  188.4 12.5 multiply_reduce_fusion.10
  206.8 11.6 multiply_reduce_fusion.3
  223.3 11.5 fusion.28
  278.0 20.9 %fusion.89 = f32[4,256,128]{2,1,0:T(8,128)} fusion(f32[4,256,24,64]{1,0,3,2:T(4,128)S(1)} %copy-done.3, f32[4,256,24]{1,2,0:T(8,128)S(1)} %bitcast.301, f32[4,1,24,128,64]{4,3,2,1,0:T(8,128)S(1)} %bitcast.268), kind=kOutput, calls=%fused_computation.126 | convolution fusion | flops 2417491968 | bytes 10059776 | tf_op jit(solution)/shard_map/transpose(jvp(vmap(ktn,khnp->kthp)))/dot_general | solution.py:77
  299.0 45.9 %fusion.11 = (f32[4,24,256]{2,1,0:T(8,128)}, f32[4,24,256]{2,1,0:T(8,128)}, f32[4,24,256]{2,1,0:T(8,128)}, f32[4,256,256]{2,1,0:T(8,128)}) fusion(f32[4,24,256]{2,1,0:T(8,128)S(1)} %copy-done.49, f32[256,256]{1,0:T(8,128)S(1)} %copy-done.43, f32[4,24,256]{2,1,0:T(8,128)S(1)} %copy-done.52, f32[4,256,256]{2,1,0:T(8,128)S(1)} %copy-done.32, ...), kind=kOutput, calls=%fused_computation.30 | convolution fusion | flops 4925874176 | bytes 15499264 | tf_op jit(solution)/shard_map/transpose(jvp(vmap(khts,kshp->kthp)))/dot_general | solution.py:63
  356.0 26.0 %while.35 = (s32[]{:T(128)}, f32[1,24,128,64]{3,2,1,0:T(8,128)S(1)}, f32[4,1,24,128,64]{4,3,2,1,0:T(8,128)}, f32[4,1,24]{2,1,0:T(1,128)S(1)}, f32[4,1,24,128,64]...) while((s32[]{:T(128)}, ...), condition=%wide.region_12.13_spmd.clone, body=%wide.region_10.12_spmd.clone.sunk | while | flops 1179628 | bytes 8652312 | solution.py:75
  382.2 12.6 fusion.80
  397.5 27.4 %bitcast_add_fusion.2 = f32[1,4,256,24,64]{2,4,3,1,0:T(8,128)} fusion(f32[4,256,24,64]{1,3,2,0:T(8,128)S(1)} %fusion.80, f32[4,256,24,64]{1,0,3,2:T(4,128)} %reshape.659, f32[24]{0:T(128)S(1)} %copy-done.93, f32[4,256,24]{1,2,0:T(8,128)S(1)} %copy-done.35, f32[4,24,256]{2,1,0:T(8,128)S(1)} %copy-done.50, f32[256,256]{1,0:T(8,128)S(1)} %copy-done.44, ...), kind=kOutput, calls=%fused_computation.66 | convolution fusion | flops 4869586944 | bytes 26837088 | tf_op jit(solution)/shard_map/transpose(jvp(vmap(khts,kshp->kthp)))/dot_general | solution.py:63
  425.0 10.1 multiply_reduce_fusion.2
  445.9 10.0 reduce-window.16
  466.3 11.1 reshape.689
  477.5 14.4 %multiply_reduce_fusion.6 = (f32[1536]{0:T(1024)S(1)}, f32[1536]{0:T(1024)S(1)}, f32[1536]{0:T(1024)S(1)}, f32[1536]{0:T(1024)S(1)}, f32[1536]{0:T(1024)S(1)}, /*index=5*/f32[1,1024,1536]{2,1,0:T(8,128)S(1)}) fusion(f32[1,1024,1536]{2,1,0:T(8,128)} %bitcast.270, f32[1024,1536]{1,0:T(8,128)} %copy-done.2, f32[1,1024,1536]{2,1,0:T(8,128)} %get-tuple-element.386, ...), kind=kLoop, calls=%fused_computation.80 | loop fusion | flops 28303872 | bytes 31488000 | tf_op jit(solution)/shard_map/transpose(jvp(vmap()))/reduce_sum | solution.py:23
  527.5 9.9 convolution_convert_fusion
  540.6 10.4 fusion.145
  566.6 138.1 %all-reduce.33.cloned.1.call-done = (f32[1024,1536]{1,0:T(8,128)}, f32[1,1024,256]{2,1,0:T(8,128)}) async-done(((f32[1024,1536]{1,0:T(8,128)}, f32[1,1024,256]{2,1,0:T(8,128)}), (f32[1024,1536]{1,0:T(8,128)}, f32[1,1024,256]{2,1,0:T(8,128)})) %all-reduce.33.cloned.1.call-update) | async-done | bytes 7340048 | tf_op jit(solution)/shard_map/psum | solution.py:190
  719.2 62.5 %all-reduce.22 = (f32[1536]{0:T(1024)}, f32[4,1536]{1,0:T(4,128)}, f32[1536]{0:T(1024)}, f32[4,256]{1,0:T(4,128)}, f32[256]{0:T(256)}, /*index=5*/f32[24]{0:T(128)}, f32[24]{0:T(128)}, f32[24]{0:T(128)}, f32[1536]{0:T(1024)}) all-reduce(f32[1536]{0:T(1024)S(1)} %get-tuple-element.314, ...), channel_id=1, replica_groups=mesh['dp'=16,'tensor'=2] {'dp'}, use_global_device_ids=true, to_apply=%region_25.26 | all-reduce | flops 12104 | bytes 96832 | tf_op jit(solution)/shard_map/psum | solution.py:217
  781.6 11.2 all-reduce.29.cloned.1.call-done
  801.9 509.1 %all-reduce.31.cloned.1.call-done = (f32[1536,1536]{1,0:T(8,128)}, f32[1536,1536]{1,0:T(8,128)}, f32[1536,24]{0,1:T(8,128)}, f32[1536,256]{1,0:T(8,128)}, f32[1536,1536]{1,0:T(8,128)}) async-done(((f32[1536,1536]{1,0:T(8,128)}, f32[1536,1536]{1,0:T(8,128)}, f32[1536,24]{0,1:T(8,128)}, f32[1536,256]{1,0:T(8,128)}, f32[1536,1536]{1,0:T(8,128)}), (f32[1536,1536]{1,0:T(8,128)}, f32[1536,1536]{1,0:T(8,128)}, ...) | async-done | bytes 30031888 | tf_op jit(solution)/shard_map/psum | solution.py:217
  (391 shorter events, 320.5 us)
Async XLA Ops:
  7.2 48.8 %copy-start = (bf16[1536,256]{1,0:T(8,128)(2,1)S(1)}, bf16[1536,256]{1,0:T(8,128)(2,1)}, u32[]{:S(2)}) copy-start(bf16[1536,256]{1,0:T(8,128)(2,1)} %param.26) | copy-start | bytes 2359300
  7.2 697.5 %all-reduce.33.cloned.1.call-start = ((), (), s32[]{:S(2)}) async-start(), calls=%async_computation.2 | async-start | bytes 14680064 | tf_op jit(solution)/shard_map/psum | solution.py:190
  134.2 33.4 %copy-start.51 = (f32[4,24,256]{2,1,0:T(8,128)}, f32[4,24,256]{2,1,0:T(8,128)S(1)}, u32[]{:S(2)}) copy-start(f32[4,24,256]{2,1,0:T(8,128)S(1)} %reduce_window_sum.55) | copy-start | bytes 294916
  206.8 28.0 %copy-start.69 = (f32[1024]{0:T(1024)}, f32[1024]{0:T(1024)S(1)}, u32[]{:S(2)}) copy-start(f32[1024]{0:T(1024)S(1)} %get-tuple-element.408) | copy-start | bytes 12292
  270.3 28.6 %slice-start.2 = ((s8[6291456]{0:T(1024)(128)(4,1)}), s8[2097152]{0:T(1024)(128)(4,1)S(1)}, s32[]{:S(2)}) async-start(s8[6291456]{0:T(1024)(128)(4,1)} %bitcast.271), calls=%async_computation.5 | async-start | bytes 4194304
  277.9 21.0 %copy-start.18 = (f32[1,4,256,24,64]{2,1,4,3,0:T(4,128)S(1)}, f32[1,4,256,24,64]{2,1,4,3,0:T(4,128)}, u32[]{:S(2)}) copy-start(f32[1,4,256,24,64]{2,1,4,3,0:T(4,128)} %reshape.662) | copy-start | bytes 18874372
  277.9 21.0 %copy-start.32 = (f32[4,256,256]{2,1,0:T(8,128)S(1)}, f32[4,256,256]{2,1,0:T(8,128)}, u32[]{:S(2)}) copy-start(f32[4,256,256]{2,1,0:T(8,128)} %copy-done.31) | copy-start | bytes 3145732
  277.9 21.0 %copy-start.43 = (f32[256,256]{1,0:T(8,128)S(1)}, f32[256,256]{1,0:T(8,128)}, u32[]{:S(2)}) copy-start(f32[256,256]{1,0:T(8,128)} %fusion.108) | copy-start | bytes 786436
  277.9 21.0 %copy-start.49 = (f32[4,24,256]{2,1,0:T(8,128)S(1)}, f32[4,24,256]{2,1,0:T(8,128)}, u32[]{:S(2)}) copy-start(f32[4,24,256]{2,1,0:T(8,128)} %get-tuple-element.418) | copy-start | bytes 294916
  277.9 21.0 %copy-start.52 = (f32[4,24,256]{2,1,0:T(8,128)S(1)}, f32[4,24,256]{2,1,0:T(8,128)}, u32[]{:S(2)}) copy-start(f32[4,24,256]{2,1,0:T(8,128)} %copy-done.51) | copy-start | bytes 294916
  277.9 21.0 %copy-start.65 = (pred[256,256]{1,0:T(8,128)(4,1)S(1)}, pred[256,256]{1,0:T(8,128)(4,1)}, u32[]{:S(2)}) copy-start(pred[256,256]{1,0:T(8,128)(4,1)} %broadcast_compare_fusion) | copy-start | bytes 196612
  382.1 42.8 %slice-start.4 = ((s8[6291456]{0:T(1024)(128)(4,1)}), s8[4194304]{0:T(1024)(128)(4,1)S(1)}, s32[]{:S(2)}) async-start(s8[6291456]{0:T(1024)(128)(4,1)} %bitcast.273), calls=%async_computation.7 | async-start | bytes 8388608
  382.2 55.2 %slice-start.6 = ((s8[6291456]{0:T(1024)(128)(4,1)}), s8[4194304]{0:T(1024)(128)(4,1)S(1)}, s32[]{:S(2)}) async-start(s8[6291456]{0:T(1024)(128)(4,1)} %bitcast.275), calls=%async_computation.9 | async-start | bytes 8388608
  397.5 27.5 %slice-start.5 = ((s8[6291456]{0:T(1024)(128)(4,1)}), s8[2097152]{0:T(1024)(128)(4,1)S(1)}, s32[]{:S(2)}) async-start(s8[6291456]{0:T(1024)(128)(4,1)} %bitcast.273), calls=%async_computation.8 | async-start | bytes 4194304
  397.5 39.9 %slice-start.7 = ((s8[6291456]{0:T(1024)(128)(4,1)}), s8[2097152]{0:T(1024)(128)(4,1)S(1)}, s32[]{:S(2)}) async-start(s8[6291456]{0:T(1024)(128)(4,1)} %bitcast.275), calls=%async_computation.10 | async-start | bytes 4194304
  526.8 266.0 %all-reduce.29.cloned.1.call-start = ((), (), s32[]{:S(2)}) async-start(), calls=%async_computation | async-start | bytes 6291456 | tf_op jit(solution)/shard_map/psum | solution.py:157
  537.5 773.5 %all-reduce.31.cloned.1.call-start = ((), (), s32[]{:S(2)}) async-start(), calls=%async_computation.1 | async-start | bytes 60063744 | tf_op jit(solution)/shard_map/psum | solution.py:217
  558.6 146.0 %copy-start.12 = (f32[1024,256]{1,0:T(8,128)S(1)}, f32[1024,256]{1,0:T(8,128)}, u32[]{:S(2)}) copy-start(f32[1024,256]{1,0:T(8,128)} %copy-done.11) | copy-start | bytes 3145732
  558.7 146.0 %copy-start.19 = (f32[1,1024,256]{2,1,0:T(8,128)S(1)}, f32[1,1024,256]{2,1,0:T(8,128)}, u32[]{:S(2)}) copy-start(f32[1,1024,256]{2,1,0:T(8,128)} %get-tuple-element.384) | copy-start | bytes 3145732
  558.7 148.1 %copy-start.79 = (f32[1,256]{1,0:T(1,128)S(1)}, f32[1,256]{1,0:T(1,128)}, u32[]{:S(2)}) copy-start(f32[1,256]{1,0:T(1,128)} %copy-done.78) | copy-start | bytes 3076
  558.7 148.1 %copy-start.81 = (f32[1,256]{1,0:T(1,128)S(1)}, f32[1,256]{1,0:T(1,128)}, u32[]{:S(2)}) copy-start(f32[1,256]{1,0:T(1,128)} %copy-done.80) | copy-start | bytes 3076
  558.7 148.1 %copy-start.83 = (f32[1,256]{1,0:T(1,128)S(1)}, f32[1,256]{1,0:T(1,128)}, u32[]{:S(2)}) copy-start(f32[1,256]{1,0:T(1,128)} %copy-done.82) | copy-start | bytes 3076
  558.7 148.1 %copy-start.85 = (f32[1,256]{1,0:T(1,128)S(1)}, f32[1,256]{1,0:T(1,128)}, u32[]{:S(2)}) copy-start(f32[1,256]{1,0:T(1,128)} %copy-done.84) | copy-start | bytes 3076
  711.9 81.0 %copy-start.77 = (f32[1024]{0:T(1024)S(1)}, f32[1024]{0:T(1024)}, u32[]{:S(2)}) copy-start(f32[1024]{0:T(1024)} %get-tuple-element.405) | copy-start | bytes 12292
  (89 other events, 829.2 us)
Sparse Core Ops, SparseCore 0:
  526.9 177.7 all-reduce.32
  707.0 85.8 all-reduce.28
  799.3 511.6 all-reduce.30
where the time goes:
time: 1350 us; the launch traced here: 1340 us
  waiting for transfers between devices  658 us (49%)
  matrix products  283 us (21%)
  local copies, waits for them, and re-layouts  176 us (13%)
  other arithmetic  134 us (10%)
  blocking collectives  73.2 us (5%)
  between operations  15.7 us (1%)
    psum x1, waiting for transfers between devices, local(): lax.psum((grad_pre_gain, grad_gate_proj, grad_value_proj, grad_step_proj,...  509 us
    psum x1, waiting for transfers between devices, local(): d_normed = lax.psum(head_terms, 'tensor') + dot_outer(state_bf, state_proj)  138 us
    dot_general x3, matrix products, mixer(): jnp.einsum('khts,kshp->kthp', weights, head_values, precision=highest)  107 us
    psum x1, blocking collectives, local(): lax.psum((grad_pre_gain, grad_gate_proj, grad_value_proj, grad_step_proj,...  62.5 us
    reshape x4, local copies, waits for them, and re-layouts, mixer(): head_values = conv_out.reshape(block_count, BLOCK, head_count, head_width)  40.7 us
    dot_general x5, matrix products, dot_outer(): lax.dot_general(left, right, (((1,), (1,)), ((), ())), preferred_element_...  40 us
    reshape x4, local copies, waits for them, and re-layouts, mixer(): mixed_out = mixed_out.reshape(length, head_count * head_width)  37.4 us
    unnamed x228, local copies, waits for them, and re-layouts  34.9 us
  transfers between devices with their start and end apart: 3, of which 3 were waited for; matrix products, arithmetic and copies ran while one was open for 5% of the time, Pallas kernels for 0%

commit v1 on v0

--- a/solution.py
+++ b/solution.py
@@ -187,7 +187,9 @@
         + dot_outer(value_bf, value_proj)
         + dot_outer(step_bf, step_proj)
     )
-    d_normed = lax.psum(head_terms, "tensor") + dot_outer(state_bf, state_proj)
+    d_normed = jnp.sum(lax.all_gather(head_terms, "tensor"), axis=0) + dot_outer(
+        state_bf, state_proj
+    )
     grad_pre_gain = jnp.sum(d_normed * input_f32 * pre_scale, axis=0)
     pre_dot = jnp.sum(d_normed * pre_gain[None, :] * input_f32, axis=1, keepdims=True)
     grad_input = (

time: 1350 us -> 1330 us (0.985)
  waiting for transfers between devices: 658 us -> 625 us
    psum x1, waiting for transfers between devices: 138 us -> 0.02 us  [local(): state_total = lax.psum(by_row(d_states), 'tensor')]
    all_gather x0 -> x1, waiting for transfers between devices: none -> 106 us  [local(): lax.all_gather(head_terms, 'tensor')]
    unnamed x228 -> x210, local copies, waits for them, and re-layouts: 34.9 us -> 28.1 us
  transfers between devices with their start and end apart: 3 -> 4, of which waited for: 3 -> 3; matrix products, arithmetic and copies ran while one was open for 5% -> 16% of each run, Pallas kernels for 0% -> 0%
where the time goes in v1:
time: 1330 us; the launch traced here: 1320 us
  waiting for transfers between devices  625 us (47%)
  matrix products  295 us (22%)
  local copies, waits for them, and re-layouts  169 us (13%)
  other arithmetic  144 us (11%)
  blocking collectives  72.5 us (5%)
  between operations  15.4 us (1%)
    psum x1, waiting for transfers between devices, local(): lax.psum((grad_pre_gain, grad_gate_proj, grad_value_proj, grad_step_proj,...  509 us
    all_gather x1, waiting for transfers between devices, local(): lax.all_gather(head_terms, 'tensor')  106 us
    dot_general x3, matrix products, mixer(): jnp.einsum('khts,kshp->kthp', weights, head_values, precision=highest)  105 us
    psum x1, blocking collectives, local(): lax.psum((grad_pre_gain, grad_gate_proj, grad_value_proj, grad_step_proj,...  61.8 us
    reshape x4, local copies, waits for them, and re-layouts, mixer(): head_values = conv_out.reshape(block_count, BLOCK, head_count, head_width)  40.8 us
    dot_general x5, matrix products, dot_outer(): lax.dot_general(left, right, (((1,), (1,)), ((), ())), preferred_element_...  39.4 us
    dot_general x3, matrix products, mixer(): jnp.einsum('ksn,khs,kshp->khnp', writer, tail_weight, head_values, precis...  38.1 us
    reshape x4, local copies, waits for them, and re-layouts, mixer(): mixed_out = mixed_out.reshape(length, head_count * head_width)  37.3 us
  transfers between devices with their start and end apart: 4, of which 3 were waited for; matrix products, arithmetic and copies ran while one was open for 16% of the time, Pallas kernels for 0%

profile of v1, /device:TPU:0, one launch (start us, length us, event | category | flops | bytes accessed | tf_op | source)
XLA Modules:
  0.0 1320.9 jit_solution(5161816531156524545)
XLA Ops:
  42.9 10.0 reshape.688
  71.4 10.3 fusion.83
  85.2 23.4 %while.34 = (s32[]{:T(128)}, f32[1,24,128,64]{3,2,1,0:T(8,128)S(1)}, f32[4,1,24,128,64]{4,3,2,1,0:T(8,128)}, f32[4,1,24,1,1]{2,4,3,1,0:T(1,128)S(1)}, f32[4,1,24...) while((s32[]{:T(128)}, f32[1,24,128,64]{3,2,1,0:T(8,128)S(1)}, ...), condition=%wide.region_4.5_spmd.clone, body=%wide.region_3.4_spmd.clone.sunk | while | flops 786435 | bytes 7865752 | solution.py:75
  134.5 33.1 %fusion.42 = f32[1,4,256,24,64]{2,4,3,1,0:T(8,128)} fusion(f32[1,4,256,24,64]{2,4,3,1,0:T(8,128)} %copy.207, f32[4,256,24,64]{1,3,2,0:T(8,128)} %bitcast.280, f32[24]{0:T(128)S(1)} %copy-done.84, f32[4,256,24]{1,2,0:T(8,128)S(1)} %bitcast.302, f32[4,24,256]{2,1,0:T(8,128)S(1)} %copy-done.42, f32[256,256]{1,0:T(8,128)S(1)} %copy-done.36, ...), kind=kOutput, calls=%fused_computation.68 | convolution fusion | flops 4869586944 | bytes 26837088 | tf_op jit(solution)/shard_map/jvp(vmap(khts,kshp->kthp))/dot_general | solution.py:63
  177.4 11.1 reshape.689
  188.5 12.4 multiply_reduce_fusion.10
  206.8 11.7 multiply_reduce_fusion.3
  223.4 14.0 %fusion.43 = (f32[1536]{0:T(1024)}, f32[1024,1536]{1,0:T(8,128)}) fusion(f32[1,1024,1536]{2,1,0:T(8,128)} %get-tuple-element.384, f32[1024,1536]{1,0:T(8,128)} %get-tuple-element.412, f32[1024]{0:T(1024)S(1)} %psum.128, f32[1024,1536]{1,0:T(8,128)} %get-tuple-element.378, f32[1024]{0:T(1024)S(1)} %get-tuple-element.405, f32[1024,1536]{1,0:T(8,128)} %get-tuple-element.413, ...), kind=kLoop, calls=%fused_computation.70 | loop fusion | flops 26737152 | bytes 31481856 | tf_op jit(solution)/shard_map/transpose(jvp(vmap()))/reduce_sum | solution.py:80
  260.4 22.8 %fusion.89 = f32[4,256,128]{2,1,0:T(8,128)S(1)} fusion(f32[4,256,24,64]{1,0,3,2:T(4,128)} %reshape.659, f32[4,256,24]{1,2,0:T(8,128)S(1)} %bitcast.303, f32[4,1,24,128,64]{4,3,2,1,0:T(8,128)} %get-tuple-element.534), kind=kOutput, calls=%fused_computation.126 | convolution fusion | flops 2417491968 | bytes 10059776 | tf_op jit(solution)/shard_map/transpose(jvp(vmap(ktn,khnp->kthp)))/dot_general | solution.py:77
  283.3 45.0 %fusion.11 = (f32[4,24,256]{2,1,0:T(8,128)}, f32[4,24,256]{2,1,0:T(8,128)}, f32[4,24,256]{2,1,0:T(8,128)}, f32[4,256,256]{2,1,0:T(8,128)S(1)}) fusion(f32[4,24,256]{2,1,0:T(8,128)S(1)} %copy-done.43, f32[256,256]{1,0:T(8,128)S(1)} %copy-done.37, f32[4,24,256]{2,1,0:T(8,128)S(1)} %copy-done.46, f32[4,256,256]{2,1,0:T(8,128)S(1)} %copy-done.27, ...), kind=kOutput, calls=%fused_computation.30 | convolution fusion | flops 4925874176 | bytes 15499264 | tf_op jit(solution)/shard_map/transpose(jvp(vmap(khts,kshp->kthp)))/dot_general | solution.py:63
  343.2 25.9 %while.35 = (s32[]{:T(128)}, f32[1,24,128,64]{3,2,1,0:T(8,128)S(1)}, f32[4,1,24,128,64]{4,3,2,1,0:T(8,128)}, f32[4,1,24]{2,1,0:T(1,128)S(1)}, f32[4,1,24,128,64]...) while((s32[]{:T(128)}, ...), condition=%wide.region_12.13_spmd.clone, body=%wide.region_10.12_spmd.clone.sunk | while | flops 1179628 | bytes 8652312 | solution.py:75
  369.2 15.3 %fusion.97 = f32[1,4,256,128]{2,3,1,0:T(8,128)S(1)} fusion(f32[1,4,256,128]{2,3,1,0:T(8,128)} %convolution_bitcast_fusion, f32[4,256,24,64]{1,0,3,2:T(4,128)} %reshape.642, f32[4,256,24]{1,2,0:T(8,128)S(1)} %copy-done.30, f32[4,1,24,128,64]{4,3,2,1,0:T(8,128)} %get-tuple-element.193), kind=kOutput, calls=%fused_computation.128 | convolution fusion | flops 2417623040 | bytes 10584064 | tf_op jit(solution)/shard_map/transpose(jvp(vmap(ksn,khs,kshp->khnp)))/dot_general | solution.py:65
  385.8 12.6 fusion.28
  403.6 12.6 fusion.80
  416.2 27.0 %bitcast_add_fusion.2 = f32[1,4,256,24,64]{2,4,3,1,0:T(8,128)} fusion(f32[4,256,24,64]{1,3,2,0:T(8,128)S(1)} %fusion.80, f32[4,256,24,64]{1,0,3,2:T(4,128)S(1)} %bitcast.277, f32[24]{0:T(128)S(1)} %copy-done.84, f32[4,256,24]{1,2,0:T(8,128)S(1)} %copy-done.30, f32[4,24,256]{2,1,0:T(8,128)S(1)} %copy-done.44, f32[256,256]{1,0:T(8,128)S(1)} %copy-done.38, ...), kind=kOutput, calls=%fused_computation.66 | convolution fusion | flops 4869586944 | bytes 26837088 | tf_op jit(solution)/shard_map/transpose(jvp(vmap(khts,kshp->kthp)))/dot_general | solution.py:63
  451.0 10.0 reduce-window.16
  471.1 11.1 reshape.690
  482.2 14.6 %multiply_reduce_fusion.6 = (f32[1536]{0:T(1024)S(1)}, f32[1536]{0:T(1024)S(1)}, f32[1536]{0:T(1024)S(1)}, f32[1536]{0:T(1024)S(1)}, f32[1536]{0:T(1024)S(1)}, /*index=5*/f32[1,1024,1536]{2,1,0:T(8,128)S(1)}) fusion(f32[1,1024,1536]{2,1,0:T(8,128)} %bitcast.269, f32[1024,1536]{1,0:T(8,128)} %copy-done.2, f32[1,1024,1536]{2,1,0:T(8,128)} %get-tuple-element.384, ...), kind=kLoop, calls=%fused_computation.80 | loop fusion | flops 28303872 | bytes 31488000 | tf_op jit(solution)/shard_map/transpose(jvp(vmap()))/reduce_sum | solution.py:23
  531.3 10.0 convolution_convert_fusion
  545.3 11.5 fusion.145
  579.7 105.9 %all-gather.3.cloned.1.call-done = f32[2048,1536]{1,0:T(8,128)} async-done(((f32[1024,1536]{1,0:T(8,128)}), f32[2048,1536]{1,0:T(8,128)}) %all-gather.3.cloned.1.call-update) | async-done | bytes 12582928 | tf_op jit(solution)/shard_map/all_gather | solution.py:190
  701.9 61.8 %all-reduce.22 = (f32[1536]{0:T(1024)}, f32[4,1536]{1,0:T(4,128)}, f32[1536]{0:T(1024)}, f32[4,256]{1,0:T(4,128)}, f32[256]{0:T(256)}, /*index=5*/f32[24]{0:T(128)}, f32[24]{0:T(128)}, f32[24]{0:T(128)}, f32[1536]{0:T(1024)}) all-reduce(f32[1536]{0:T(1024)S(1)} %get-tuple-element.314, ...), channel_id=1, replica_groups=mesh['dp'=16,'tensor'=2] {'dp'}, use_global_device_ids=true, to_apply=%region_25.26 | all-reduce | flops 12104 | bytes 96832 | tf_op jit(solution)/shard_map/psum | solution.py:219
  763.7 10.1 all-reduce.28.cloned.1.call-done
  782.8 508.9 %all-reduce.32.cloned.1.call-done = (f32[1536,1536]{1,0:T(8,128)}, f32[1536,1536]{1,0:T(8,128)}, f32[1536,24]{0,1:T(8,128)}, f32[1536,256]{1,0:T(8,128)}, f32[1536,1536]{1,0:T(8,128)}) async-done(((f32[1536,1536]{1,0:T(8,128)}, f32[1536,1536]{1,0:T(8,128)}, f32[1536,24]{0,1:T(8,128)}, f32[1536,256]{1,0:T(8,128)}, f32[1536,1536]{1,0:T(8,128)}), (f32[1536,1536]{1,0:T(8,128)}, f32[1536,1536]{1,0:T(8,128)}, ...) | async-done | bytes 30031888 | tf_op jit(solution)/shard_map/psum | solution.py:219
  (377 shorter events, 323.6 us)
Async XLA Ops:
  7.2 48.9 %copy-start = (bf16[1536,256]{1,0:T(8,128)(2,1)S(1)}, bf16[1536,256]{1,0:T(8,128)(2,1)}, u32[]{:S(2)}) copy-start(bf16[1536,256]{1,0:T(8,128)(2,1)} %param.26) | copy-start | bytes 2359300
  7.2 565.3 %all-reduce.30.cloned.1.call-start = ((), (), s32[]{:S(2)}) async-start(), calls=%async_computation.1 | async-start | bytes 2097152 | tf_op jit(solution)/shard_map/psum | solution.py:179
  134.5 33.1 %copy-start.45 = (f32[4,24,256]{2,1,0:T(8,128)}, f32[4,24,256]{2,1,0:T(8,128)S(1)}, u32[]{:S(2)}) copy-start(f32[4,24,256]{2,1,0:T(8,128)S(1)} %reduce_window_sum.55) | copy-start | bytes 294916
  252.1 31.2 %slice-start = ((s8[6291456]{0:T(1024)(128)(4,1)}), s8[2097152]{0:T(1024)(128)(4,1)S(1)}, s32[]{:S(2)}) async-start(s8[6291456]{0:T(1024)(128)(4,1)} %bitcast.270), calls=%async_computation.4 | async-start | bytes 4194304
  260.3 22.9 %slice-start.1 = ((s8[6291456]{0:T(1024)(128)(4,1)}), s8[4194304]{0:T(1024)(128)(4,1)S(1)}, s32[]{:S(2)}) async-start(s8[6291456]{0:T(1024)(128)(4,1)} %bitcast.270), calls=%async_computation.5 | async-start | bytes 8388608
  260.3 22.9 %copy-start.14 = (f32[1,4,256,24,64]{2,1,4,3,0:T(4,128)S(1)}, f32[1,4,256,24,64]{2,1,4,3,0:T(4,128)}, u32[]{:S(2)}) copy-start(f32[1,4,256,24,64]{2,1,4,3,0:T(4,128)} %reshape.662) | copy-start | bytes 18874372
  260.3 22.9 %copy-start.27 = (f32[4,256,256]{2,1,0:T(8,128)S(1)}, f32[4,256,256]{2,1,0:T(8,128)}, u32[]{:S(2)}) copy-start(f32[4,256,256]{2,1,0:T(8,128)} %copy-done.26) | copy-start | bytes 3145732
  260.3 22.9 %copy-start.37 = (f32[256,256]{1,0:T(8,128)S(1)}, f32[256,256]{1,0:T(8,128)}, u32[]{:S(2)}) copy-start(f32[256,256]{1,0:T(8,128)} %fusion.108) | copy-start | bytes 786436
  260.3 22.9 %copy-start.43 = (f32[4,24,256]{2,1,0:T(8,128)S(1)}, f32[4,24,256]{2,1,0:T(8,128)}, u32[]{:S(2)}) copy-start(f32[4,24,256]{2,1,0:T(8,128)} %get-tuple-element.416) | copy-start | bytes 294916
  260.4 22.9 %copy-start.46 = (f32[4,24,256]{2,1,0:T(8,128)S(1)}, f32[4,24,256]{2,1,0:T(8,128)}, u32[]{:S(2)}) copy-start(f32[4,24,256]{2,1,0:T(8,128)} %copy-done.45) | copy-start | bytes 294916
  260.4 22.9 %copy-start.59 = (pred[256,256]{1,0:T(8,128)(4,1)S(1)}, pred[256,256]{1,0:T(8,128)(4,1)}, u32[]{:S(2)}) copy-start(pred[256,256]{1,0:T(8,128)(4,1)} %broadcast_compare_fusion) | copy-start | bytes 196612
  283.2 48.9 %slice-start.4 = ((s8[6291456]{0:T(1024)(128)(4,1)}), s8[4194304]{0:T(1024)(128)(4,1)S(1)}, s32[]{:S(2)}) async-start(s8[6291456]{0:T(1024)(128)(4,1)} %bitcast.274), calls=%async_computation.8 | async-start | bytes 8388608
  283.3 45.0 %copy-start.13 = (f32[1,1024,128]{2,1,0:T(8,128)S(1)}, f32[1,1024,128]{2,1,0:T(8,128)}, u32[]{:S(2)}) copy-start(f32[1,1024,128]{2,1,0:T(8,128)} %get-tuple-element.398) | copy-start | bytes 1572868
  283.3 48.8 %slice-start.5 = ((s8[6291456]{0:T(1024)(128)(4,1)}), s8[2097152]{0:T(1024)(128)(4,1)S(1)}, s32[]{:S(2)}) async-start(s8[6291456]{0:T(1024)(128)(4,1)} %bitcast.274), calls=%async_computation.9 | async-start | bytes 4194304
  343.2 26.0 %copy-start.30 = (f32[4,256,24]{1,2,0:T(8,128)S(1)}, f32[4,256,24]{1,2,0:T(8,128)}, u32[]{:S(2)}) copy-start(f32[4,256,24]{1,2,0:T(8,128)} %copy-done.29) | copy-start | bytes 294916
  385.8 299.9 %all-gather.3.cloned.1.call-start = ((), (), s32[]{:S(2)}) async-start(), calls=%async_computation.2 | async-start | bytes 18874368 | tf_op jit(solution)/shard_map/all_gather | solution.py:190
  403.5 39.7 %slice-start.2 = ((s8[6291456]{0:T(1024)(128)(4,1)}), s8[4194304]{0:T(1024)(128)(4,1)S(1)}, s32[]{:S(2)}) async-start(s8[6291456]{0:T(1024)(128)(4,1)} %bitcast.272), calls=%async_computation.6 | async-start | bytes 8388608
  416.2 27.0 %slice-start.3 = ((s8[6291456]{0:T(1024)(128)(4,1)}), s8[2097152]{0:T(1024)(128)(4,1)S(1)}, s32[]{:S(2)}) async-start(s8[6291456]{0:T(1024)(128)(4,1)} %bitcast.272), calls=%async_computation.7 | async-start | bytes 4194304
  531.2 242.6 %all-reduce.28.cloned.1.call-start = ((), (), s32[]{:S(2)}) async-start(), calls=%async_computation | async-start | bytes 6291456 | tf_op jit(solution)/shard_map/psum | solution.py:157
  541.2 750.5 %all-reduce.32.cloned.1.call-start = ((), (), s32[]{:S(2)}) async-start(), calls=%async_computation.3 | async-start | bytes 60063744 | tf_op jit(solution)/shard_map/psum | solution.py:219
  545.3 19.1 %slice-start.8 = ((s8[6291456]{0:T(1024)(128)(4,1)}), s8[4194304]{0:T(1024)(128)(4,1)S(1)}, s32[]{:S(2)}) async-start(s8[6291456]{0:T(1024)(128)(4,1)} %bitcast.278), calls=%async_computation.12 | async-start | bytes 8388608
  695.3 78.5 %copy-start.68 = (f32[1024]{0:T(1024)S(1)}, f32[1024]{0:T(1024)}, u32[]{:S(2)}) copy-start(f32[1024]{0:T(1024)} %get-tuple-element.403) | copy-start | bytes 12292
  1291.7 18.7 %slice-start.10 = ((s8[9437184]{0:T(1024)(128)(4,1)}), s8[4194304]{0:T(1024)(128)(4,1)S(1)}, s32[]{:S(2)}) async-start(s8[9437184]{0:T(1024)(128)(4,1)} %bitcast.294), calls=%async_computation.14 | async-start | bytes 8388608
  1291.7 18.7 %slice-start.11 = ((s8[9437184]{0:T(1024)(128)(4,1)}), s8[4194304]{0:T(1024)(128)(4,1)S(1)}, s32[]{:S(2)}) async-start(s8[9437184]{0:T(1024)(128)(4,1)} %bitcast.294), calls=%async_computation.15 | async-start | bytes 8388608
  (81 other events, 726.9 us)
Sparse Core Ops, SparseCore 0:
  385.9 41.8 all-reduce.29
  531.3 154.2 all-gather.2
  687.9 85.8 all-reduce.27
  780.1 511.6 all-reduce.31
